TPU v7x, 256 devices: a whole 4x4x8 slice. The times are simulated.
256 devices in a mesh: seq: 16 (over z, core), dp: 16 (over y, x).
Axes of the slice: x: 4, y: 4, z: 8, core: 2. Of those that a mesh axis runs over, the one named last changes fastest.
Arguments:
- queries: bfloat16 [16, 2048, 1280], P('dp', 'seq'), may hold values from -43 to 43
- key_rows: bfloat16 [16, 2048, 1280], P('dp', 'seq'), may hold values from -7 to 7
- value_rows: bfloat16 [16, 2048, 1280], P('dp', 'seq'), may hold values from -6 to 6
- resid_in: bfloat16 [16, 2048, 1280], P('dp', 'seq'), may hold values from -6 to 6
- llm_grad: bfloat16 [16, 3072, 1280], P('dp', 'seq'), may hold values from -6 to 6
- vision_slot: int32 [16, 3072], P('dp', 'seq'), may hold values from -1 to 2047, as said below
- window_mask: int32 [16, 32, 2], P('dp', 'seq'), may hold values from 0 to 1, as said below
- w_up: bfloat16 [1280, 2560], P('dp'), may hold values from -0.15625 to 0.15625
- w_down: bfloat16 [2560, 1280], P('dp'), may hold values from -0.125 to 0.125
- norm_gain: bfloat16 [1280], P('dp'), may hold values from 0.25 to 1.75
Outputs:
- grad_query: bfloat16 [16, 2048, 1280], P('dp', 'seq')
- grad_key: bfloat16 [16, 2048, 1280], P('dp', 'seq')
- grad_value: bfloat16 [16, 2048, 1280], P('dp', 'seq')
- grad_resid: bfloat16 [16, 2048, 1280], P('dp', 'seq')
- grad_up: bfloat16 [1280, 2560], P('seq', 'dp')
- grad_down: bfloat16 [2560, 1280], P('seq', 'dp')
- grad_gain: float32 [1280], replicated
Inputs may be any that keep to these rules, and one draw needn't show every extreme that they name: `vision_slot`: -1 marks a text position; every vision token of a batch stands at exactly one position. Positions come in aligned runs of 16: each run is text or the 16 consecutive vision tokens of one tile, in order. Each language-model shard holds exactly 8 tiles, and at most 32 vision tokens of one owner; in every batch, for every owner, some shard holds exactly 32 of that owner's vision tokens. `window_mask`: each owner's 2 blocks are split into images of one or more consecutive blocks; a block attends to exactly the blocks of its own image, itself included (entry i % 2 of row i is 1).
All inputs are finite; a program needn't handle non-finite values.
Results may differ from a plain program's by a relative error of at most 0.023.
Values may be sent and summed in bfloat16 or wider, within the bound.
A program may use at most 128 MiB of HBM per device.

v0:
```python
import math
import jax
import jax.numpy as jnp
from jax import lax
from jax.sharding import PartitionSpec as P

HEADS = 16
HDIM = 80
BLK = 64
PIECE = 16


def contract(left, right, left_dim, right_dim):
    return lax.dot_general(
        left, right, (((left_dim,), (right_dim,)), ((), ())), preferred_element_type=jnp.float32
    )


def per_device(
    queries,
    key_rows,
    value_rows,
    resid_in,
    llm_grad,
    vision_slot,
    window_mask,
    w_up,
    w_down,
    norm_gain,
):
    seq_count = lax.axis_size("seq")
    data_count = lax.axis_size("dp")
    query = queries[0]
    key_block = key_rows[0]
    value_block = value_rows[0]
    tokens, feat_dim = query.shape
    att_scale = 1.0 / math.sqrt(HDIM)
    up_full, down_full, gain_full = (
        lax.all_gather(w_up, "dp", axis=0, tiled=True),
        lax.all_gather(w_down, "dp", axis=0, tiled=True),
        lax.all_gather(norm_gain, "dp", axis=0, tiled=True),
    )
    slot_ids = vision_slot[0]
    piece_count = tokens // PIECE
    capacity = PIECE * (1 + (piece_count + seq_count - 2) // seq_count)
    owner_of = jnp.where(slot_ids >= 0, slot_ids // tokens, seq_count)
    onehot = (owner_of[:, None] == jnp.arange(seq_count)[None, :]).astype(jnp.int32)
    ranking = jnp.sum((jnp.cumsum(onehot, axis=0) - 1) * onehot, axis=1)
    target = jnp.where(slot_ids >= 0, owner_of * capacity + ranking, seq_count * capacity)
    send_rows = (
        jnp.zeros((seq_count * capacity, feat_dim), jnp.bfloat16)
        .at[target]
        .set(llm_grad[0], mode="drop")
    )
    send_ids = (
        jnp.full((seq_count * capacity,), -1, jnp.int32)
        .at[target]
        .set(jnp.where(slot_ids >= 0, slot_ids % tokens, -1), mode="drop")
    )
    recv_rows = lax.all_to_all(
        send_rows.reshape(seq_count, capacity, feat_dim),
        "seq",
        split_axis=0,
        concat_axis=0,
        tiled=True,
    )
    recv_ids = lax.all_to_all(
        send_ids.reshape(seq_count, capacity), "seq", split_axis=0, concat_axis=0, tiled=True
    )
    flat_ids = recv_ids.reshape(seq_count * capacity)
    landing = jnp.where(flat_ids >= 0, flat_ids, tokens)
    grad_rows = (
        jnp.zeros((tokens, feat_dim), jnp.bfloat16)
        .at[landing]
        .set(recv_rows.reshape(seq_count * capacity, feat_dim), mode="drop")
    )
    allowed = jnp.repeat(jnp.repeat(window_mask[0] > 0, BLK, axis=0), BLK, axis=1)
    q_heads = query.reshape(tokens, HEADS, HDIM)
    k_heads = key_block.reshape(tokens, HEADS, HDIM)
    v_heads = value_block.reshape(tokens, HEADS, HDIM)
    scores = (
        jnp.einsum("qhd,khd->hqk", q_heads, k_heads, preferred_element_type=jnp.float32) * att_scale
    )
    masked = jnp.where(allowed[None], scores, -jnp.inf)
    highest = jnp.max(masked, axis=2, keepdims=True)
    exp_terms = jnp.where(allowed[None], jnp.exp(masked - highest), 0.0)
    attn_probs = exp_terms / jnp.sum(exp_terms, axis=2, keepdims=True)
    probs_low = attn_probs.astype(jnp.bfloat16)
    attn_heads = jnp.einsum(
        "hqk,khd->qhd", probs_low, v_heads, preferred_element_type=jnp.float32
    ).astype(jnp.bfloat16)
    attn_out = attn_heads.reshape(tokens, feat_dim)
    hidden = resid_in[0].astype(jnp.float32) + attn_out.astype(jnp.float32)
    center = jnp.mean(hidden, axis=1, keepdims=True)
    variance = jnp.mean(jnp.square(hidden - center), axis=1, keepdims=True)
    inverse = lax.rsqrt(variance + 1e-06)
    normal_unit = (hidden - center) * inverse
    gain_wide = gain_full.astype(jnp.float32)
    normed = (normal_unit * gain_wide).astype(jnp.bfloat16)
    pre_act = jnp.dot(normed, up_full, preferred_element_type=jnp.float32)
    sig_gate = jax.nn.sigmoid(1.702 * pre_act)
    act_low = (pre_act * sig_gate).astype(jnp.bfloat16)
    down_term = contract(act_low, grad_rows, 0, 0)
    d_act = contract(grad_rows, down_full, 1, 1)
    d_pre = (d_act * (sig_gate + 1.702 * pre_act * sig_gate * (1.0 - sig_gate))).astype(
        jnp.bfloat16
    )
    d_normed = contract(d_pre, up_full, 1, 1)
    gain_term = jnp.sum(d_normed * normal_unit, axis=0)
    d_unit = d_normed * gain_wide
    d_hidden = inverse * (
        d_unit
        - jnp.mean(d_unit, axis=1, keepdims=True)
        - normal_unit * jnp.mean(d_unit * normal_unit, axis=1, keepdims=True)
    )
    grad_resid = (grad_rows.astype(jnp.float32) + d_hidden).astype(jnp.bfloat16)
    up_term = contract(normed, d_pre, 0, 0)
    grad_heads = grad_resid.reshape(tokens, HEADS, HDIM)
    grad_value = jnp.einsum(
        "hqk,qhd->khd", probs_low, grad_heads, preferred_element_type=jnp.float32
    ).astype(jnp.bfloat16)
    d_probs = jnp.einsum("qhd,khd->hqk", grad_heads, v_heads, preferred_element_type=jnp.float32)
    delta = jnp.einsum("qhd,qhd->hq", grad_heads, attn_heads, preferred_element_type=jnp.float32)
    d_scores = (attn_probs * (d_probs - delta[:, :, None]) * att_scale).astype(jnp.bfloat16)
    grad_query = jnp.einsum(
        "hqk,khd->qhd", d_scores, k_heads, preferred_element_type=jnp.float32
    ).astype(jnp.bfloat16)
    grad_key = jnp.einsum(
        "hqk,qhd->khd", d_scores, q_heads, preferred_element_type=jnp.float32
    ).astype(jnp.bfloat16)
    up_part, down_part = (
        lax.psum_scatter(
            up_term.astype(jnp.bfloat16), "seq", scatter_dimension=0, tiled=True
        ).astype(jnp.float32),
        lax.psum_scatter(
            down_term.astype(jnp.bfloat16), "seq", scatter_dimension=0, tiled=True
        ).astype(jnp.float32),
    )
    up_panel, down_panel = (
        lax.psum_scatter(
            up_part.astype(jnp.bfloat16), "dp", scatter_dimension=1, tiled=True
        ).astype(jnp.float32),
        lax.psum_scatter(
            down_part.astype(jnp.bfloat16), "dp", scatter_dimension=1, tiled=True
        ).astype(jnp.float32),
    )
    factor = 1.0 / math.sqrt(data_count * seq_count * tokens)
    gain_total = lax.psum(gain_term, ("seq", "dp"))
    return (
        grad_query.reshape(1, tokens, feat_dim),
        grad_key.reshape(1, tokens, feat_dim),
        grad_value.reshape(1, tokens, feat_dim),
        grad_resid[None],
        (up_panel * factor).astype(jnp.bfloat16),
        (down_panel * factor).astype(jnp.bfloat16),
        gain_total * factor,
    )


def solution(mesh):
    in_specs = (
        P("dp", "seq", None),
        P("dp", "seq", None),
        P("dp", "seq", None),
        P("dp", "seq", None),
        P("dp", "seq", None),
        P("dp", "seq"),
        P("dp", "seq", None),
        P("dp", None),
        P("dp", None),
        P("dp"),
    )
    out_specs = (
        P("dp", "seq", None),
        P("dp", "seq", None),
        P("dp", "seq", None),
        P("dp", "seq", None),
        P("seq", "dp"),
        P("seq", "dp"),
        P(),
    )
    return jax.shard_map(
        per_device, mesh=mesh, in_specs=in_specs, out_specs=out_specs, check_vma=False
    )
```

profile of v0, /device:TPU:2, one launch (start us, length us, event | category | flops | bytes accessed | tf_op | source)
XLA Modules:
  0.0 466.7 jit_solution(10220901300629912734)
XLA Ops:
  11.0 1.2 scatter_custom_fusion
  12.9 8.6 %all-to-all-start = ((s32[16,1,32]{2,1,0:T(1,128)}), s32[16,1,32]{2,1,0:T(1,128)S(1)}, u32[]{:S(2)}, u32[]{:S(2)}) async-start(s32[16,1,32]{2,1,0:T(1,128)} %all_to_all.9), calls=%async_computation | async-start | bytes 16384 | tf_op jit(solution)/shard_map/all_to_all | solution.py:67
  21.5 2.7 scatter_custom_fusion.1
  24.1 4.9 %all-to-all-done = s32[16,1,32]{2,1,0:T(1,128)S(1)} async-done(((s32[16,1,32]{2,1,0:T(1,128)}), s32[16,1,32]{2,1,0:T(1,128)S(1)}, u32[]{:S(2)}, u32[]{:S(2)}) %all-to-all-start) | async-done | bytes 2080 | tf_op jit(solution)/shard_map/all_to_all | solution.py:67
  29.0 3.8 all-to-all-start.1
  34.4 1.5 fusion.35
  35.9 1.6 convolution_convert_fusion.3
  40.4 37.7 %all-reduce.1 = bf16[1280]{0:T(1024)(128)(2,1)S(1)} all-reduce(bf16[1280]{0:T(1024)(128)(2,1)S(1)} %dynamic-update-slice), channel_id=1, replica_groups=mesh['seq'=16,'dp'=16] {'dp'}, use_global_device_ids=true, to_apply=%add.1 | all-reduce | flops 1280 | bytes 5120
  79.7 2.9 scatter_custom_fusion.2
  82.7 3.9 fusion.31
  86.6 64.3 %all-gather.3.cloned.1.call-done = bf16[2560,1280]{1,0:T(8,128)(2,1)} async-done(((bf16[160,1280]{1,0:T(8,128)(2,1)}), bf16[2560,1280]{1,0:T(8,128)(2,1)}) %all-gather.3.cloned.1.call-update) | async-done | bytes 6553616 | tf_op jit(solution)/shard_map/all_gather | solution.py:40
  151.0 5.1 %fusion.1 = bf16[128,2560]{1,0:T(8,128)(2,1)S(1)} fusion(bf16[128,1280]{1,0:T(8,128)(2,1)S(1)} %scatter_custom_fusion.2, bf16[2560,1280]{1,0:T(8,128)(2,1)} %all-gather.3.cloned.1.call-done, f32[128,2560]{1,0:T(8,128)S(1)} %fusion.31), kind=kOutput, calls=%fused_computation.7 | convolution fusion | flops 842137600 | bytes 8847360 | tf_op jit(solution)/shard_map/dot_general | solution.py:14
  156.1 4.7 convolution_convert_fusion.1
  160.8 4.6 convolution_convert_fusion
  165.5 5.2 %multiply_reduce_fusion = (f32[1280]{0:T(1024)S(1)}, f32[128]{0:T(128)S(1)}, f32[128]{0:T(128)S(1)}, f32[128,1280]{1,0:T(8,128)S(1)}) fusion(f32[128,1280]{1,0:T(8,128)S(1)} %get-tuple-element.32, f32[128]{0:T(128)S(1)} %add_rsqrt_fusion, f32[128]{0:T(128)S(1)} %broadcast_multiply_fusion.3, f32[1280]{0:T(1024)S(1)} %convert_element_type.92, ...), kind=kOutput, calls=%fused_computation.26 | convolution fusion | flops 840169984 | bytes 8531968 | tf_op jit(solution)/shard_map/dot_general | solution.py:14
  170.7 57.6 %reduce-scatter.9.cloned.1.call-done = bf16[80,2560]{1,0:T(8,128)(2,1)} async-done(((bf16[1280,2560]{1,0:T(8,128)(2,1)}), bf16[80,2560]{1,0:T(8,128)(2,1)}) %reduce-scatter.9.cloned.1.call-update) | async-done | bytes 409616 | tf_op jit(solution)/shard_map/reduce_scatter | solution.py:132
  228.3 2.1 copy.80
  231.5 1.7 fusion.8
  233.6 63.2 %reduce-scatter.11.cloned.1.call-done = bf16[160,1280]{1,0:T(8,128)(2,1)} async-done(((bf16[2560,1280]{1,0:T(8,128)(2,1)}), bf16[160,1280]{1,0:T(8,128)(2,1)}) %reduce-scatter.11.cloned.1.call-update) | async-done | bytes 409616 | tf_op jit(solution)/shard_map/reduce_scatter | solution.py:135
  296.7 2.1 copy.82
  299.4 0.9 copy.64
  301.7 0.9 copy.66
  302.6 75.3 %psum.7 = f32[1280]{0:T(1024)S(1)} all-reduce(f32[1280]{0:T(1024)S(1)} %get-tuple-element.28), channel_id=1, replica_groups=mesh['seq'=16,'dp'=16] {'seq','dp'}, use_global_device_ids=true, to_apply=%region_17.18 | all-reduce | flops 1280 | bytes 10240 | tf_op jit(solution)/shard_map/psum | solution.py:148
  380.0 78.3 %reduce-scatter.15.cloned.1.call-done = bf16[80,160]{1,0:T(8,128)(2,1)} async-done(((bf16[1280,160]{1,0:T(8,128)(2,1)}), bf16[80,160]{1,0:T(8,128)(2,1)}) %reduce-scatter.15.cloned.1.call-update) | async-done | bytes 25616
  (97 shorter events, 16.9 us)
Async XLA Ops:
  7.2 14.3 %copy-start = (bf16[1,192,1280]{2,1,0:T(8,128)(2,1)S(1)}, bf16[1,192,1280]{2,1,0:T(8,128)(2,1)}, u32[]{:S(2)}) copy-start(bf16[1,192,1280]{2,1,0:T(8,128)(2,1)} %param.14) | copy-start | bytes 1474564
  7.2 75.5 %all-gather.5.cloned.1.call-start = ((), (), s32[]{:S(2)}) async-start(), calls=%async_computation.7 | async-start | bytes 6963200 | tf_op jit(solution)/shard_map/all_gather | solution.py:39
  7.9 143.1 %all-gather.3.cloned.1.call-start = ((), (), s32[]{:S(2)}) async-start(), calls=%async_computation.6 | async-start | bytes 6963200 | tf_op jit(solution)/shard_map/all_gather | solution.py:40
  12.9 16.1 %all-to-all-start = ((s32[16,1,32]{2,1,0:T(1,128)}), s32[16,1,32]{2,1,0:T(1,128)S(1)}, u32[]{:S(2)}, u32[]{:S(2)}) async-start(s32[16,1,32]{2,1,0:T(1,128)} %all_to_all.9), calls=%async_computation | async-start | bytes 16384 | tf_op jit(solution)/shard_map/all_to_all | solution.py:67
  29.0 3.9 copy-start.8
  29.0 4.1 copy-start.9
  29.0 50.7 %all-to-all-start.1 = ((bf16[16,32,1280]{2,1,0:T(8,128)(2,1)}), bf16[16,32,1280]{2,1,0:T(8,128)(2,1)S(1)}, u32[]{:S(2)}, u32[]{:S(2)}) async-start(bf16[16,32,1280]{2,1,0:T(8,128)(2,1)} %bitcast.13), calls=%async_computation.1 | async-start | bytes 2621440 | tf_op jit(solution)/shard_map/all_to_all | solution.py:60
  32.8 1.0 copy-start.10
  32.9 1.2 copy-start.14
  32.9 195.4 %reduce-scatter.9.cloned.1.call-start = ((), (), s32[]{:S(2)}) async-start(), calls=%async_computation.8 | async-start | bytes 6963200 | tf_op jit(solution)/shard_map/reduce_scatter | solution.py:132
  33.2 2.7 copy-start.3
  33.8 2.0 copy-start.11
  34.0 1.8 copy-start.1
  38.2 1.9 copy-start.15
  38.3 39.8 %copy-start.13 = (bf16[1,128,1280]{2,1,0:T(8,128)(2,1)S(1)}, bf16[1,128,1280]{2,1,0:T(8,128)(2,1)}, u32[]{:S(2)}) copy-start(bf16[1,128,1280]{2,1,0:T(8,128)(2,1)} %param.13) | copy-start | bytes 983044
  160.8 136.0 %reduce-scatter.11.cloned.1.call-start = ((), (), s32[]{:S(2)}) async-start(), calls=%async_computation.9 | async-start | bytes 6963200 | tf_op jit(solution)/shard_map/reduce_scatter | solution.py:135
  165.5 213.0 %reduce-scatter.13.cloned.1.call-start = ((), (), s32[]{:S(2)}) async-start(), calls=%async_computation.10 | async-start | bytes 696320
  230.4 228.0 %reduce-scatter.15.cloned.1.call-start = ((), (), s32[]{:S(2)}) async-start(), calls=%async_computation.11 | async-start | bytes 696320
  230.4 1.0 copy-start.7
  230.4 1.1 copy-start.12
  230.8 2.4 copy-start.5
  231.5 1.7 copy-start.4
  233.2 65.6 %copy-start.2 = (bf16[1,128,1280]{1,2,0:T(8,128)(2,1)S(1)}, bf16[1,128,1280]{1,2,0:T(8,128)(2,1)}, u32[]{:S(2)}) copy-start(bf16[1,128,1280]{1,2,0:T(8,128)(2,1)} %copy-done.1) | copy-start | bytes 983044
  298.9 2.3 copy-start.17
  (2 other events, 1.4 us)
Sparse Core Ops, SparseCore 0:
  10.4 70.4 all-gather.4
  83.3 67.5 all-gather.2
  160.9 67.3 reduce-scatter.8
  230.7 65.9 reduce-scatter.10
  300.1 76.7 reduce-scatter.12
  380.2 78.0 reduce-scatter.14
where the time goes:
time: 467 us
  waiting for transfers between devices  270 us (58%)
  blocking collectives  113 us (24%)
  matrix products  29.6 us (6%)
  local copies, waits for them, and re-layouts  21.1 us (5%)
  between operations  15.1 us (3%)
  starting transfers between devices  12.6 us (3%)
  other arithmetic  5.58 us (1%)
    unnamed x8, waiting for transfers between devices  79.8 us
    psum x1, blocking collectives, per_device(): gain_total = lax.psum(gain_term, ('seq', 'dp'))  75.3 us
    all_gather x1, waiting for transfers between devices, per_device(): lax.all_gather(w_down, 'dp', axis=0, tiled=True)  64.3 us
    reduce_scatter x1, waiting for transfers between devices, per_device(): lax.psum_scatter(down_term.astype(jnp.bfloat16), 'seq', scatter_dimension...  63.2 us
    reduce_scatter x1, waiting for transfers between devices, per_device(): lax.psum_scatter(up_term.astype(jnp.bfloat16), 'seq', scatter_dimension=0...  57.6 us
    unnamed x1, blocking collectives  37.7 us
    dot_general x4, matrix products, contract(): lax.dot_general(left, right, (((left_dim,), (right_dim,)), ((), ())), pre...  19.6 us
    unnamed x49, local copies, waits for them, and re-layouts  12.1 us
  transfers between devices with their start and end apart: 8, of which 5 were waited for; matrix products, arithmetic and copies ran while one was open for 9% of the time, Pallas kernels for 0%

commit v1 on v0

--- a/solution.py
+++ b/solution.py
@@ -37,7 +37,9 @@
     att_scale = 1.0 / math.sqrt(HDIM)
     up_full, down_full, gain_full = (
         lax.all_gather(w_up, "dp", axis=0, tiled=True),
-        lax.all_gather(w_down, "dp", axis=0, tiled=True),
+        jnp.concatenate(
+            lax.all_to_all(jnp.stack([w_down] * lax.axis_size("dp")), "dp", 0, 0), axis=0
+        ),
         lax.all_gather(norm_gain, "dp", axis=0, tiled=True),
     )
     slot_ids = vision_slot[0]

time: 467 us -> 527 us (1.13)
  blocking collectives: 113 us -> 230 us
  waiting for transfers between devices: 270 us -> 206 us
    unnamed x1, blocking collectives: 37.7 us -> 118 us
    all_gather x1 -> x0, waiting for transfers between devices: 64.3 us -> none  [per_device(): lax.all_gather(w_down, 'dp', axis=0, tiled=True)]
    all_to_all x0 -> x1, blocking collectives: none -> 36.3 us  [per_device(): lax.all_to_all(send_rows.reshape(seq_count, capacity, feat_dim), 'seq', s...]
    unnamed x8 -> x7, waiting for transfers between devices: 79.8 us -> 79.2 us
    unnamed x49 -> x51, local copies, waits for them, and re-layouts: 12.1 us -> 12.1 us
  transfers between devices with their start and end apart: 8 -> 7, of which waited for: 5 -> 4; matrix products, arithmetic and copies ran while one was open for 9% -> 8% of each run, Pallas kernels for 0% -> 0%
where the time goes in v1:
time: 527 us
  blocking collectives  230 us (44%)
  waiting for transfers between devices  206 us (39%)
  matrix products  29.5 us (6%)
  local copies, waits for them, and re-layouts  23.6 us (4%)
  starting transfers between devices  16.4 us (3%)
  between operations  14.8 us (3%)
  other arithmetic  5.58 us (1%)
    unnamed x1, blocking collectives  118 us
    unnamed x7, waiting for transfers between devices  79.2 us
    psum x1, blocking collectives, per_device(): gain_total = lax.psum(gain_term, ('seq', 'dp'))  75.6 us
    reduce_scatter x1, waiting for transfers between devices, per_device(): lax.psum_scatter(down_term.astype(jnp.bfloat16), 'seq', scatter_dimension...  63.5 us
    reduce_scatter x1, waiting for transfers between devices, per_device(): lax.psum_scatter(up_term.astype(jnp.bfloat16), 'seq', scatter_dimension=0...  58 us
    all_to_all x1, blocking collectives, per_device(): lax.all_to_all(send_rows.reshape(seq_count, capacity, feat_dim), 'seq', s...  36.3 us
    dot_general x4, matrix products, contract(): lax.dot_general(left, right, (((left_dim,), (right_dim,)), ((), ())), pre...  19.6 us
    unnamed x51, local copies, waits for them, and re-layouts  12.1 us
  transfers between devices with their start and end apart: 7, of which 4 were waited for; matrix products, arithmetic and copies ran while one was open for 8% of the time, Pallas kernels for 0%

profile of v1, /device:TPU:2, one launch (start us, length us, event | category | flops | bytes accessed | tf_op | source)
XLA Modules:
  0.0 526.5 jit_solution(5458158378696916960)
XLA Ops:
  10.3 1.2 scatter_custom_fusion
  12.1 8.6 %all-to-all-start = ((s32[16,1,32]{2,1,0:T(1,128)}), s32[16,1,32]{2,1,0:T(1,128)S(1)}, u32[]{:S(2)}, u32[]{:S(2)}) async-start(s32[16,1,32]{2,1,0:T(1,128)} %all_to_all.12), calls=%async_computation | async-start | bytes 16384 | tf_op jit(solution)/shard_map/all_to_all | solution.py:69
  20.7 1.9 scatter_custom_fusion.1
  22.6 5.6 %all-to-all-done = s32[16,1,32]{2,1,0:T(1,128)S(1)} async-done(((s32[16,1,32]{2,1,0:T(1,128)}), s32[16,1,32]{2,1,0:T(1,128)S(1)}, u32[]{:S(2)}, u32[]{:S(2)}) %all-to-all-start) | async-done | bytes 2080 | tf_op jit(solution)/shard_map/all_to_all | solution.py:69
  28.2 36.3 %all_to_all.19 = bf16[16,32,1280]{2,1,0:T(8,128)(2,1)S(1)} all-to-all(bf16[16,32,1280]{2,1,0:T(8,128)(2,1)S(1)} %bitcast.88), channel_id=1, replica_groups=mesh['seq'=16,'dp'=16] {'seq'}, dimensions={0} | all-to-all | bytes 2621440 | tf_op jit(solution)/shard_map/all_to_all | solution.py:62
  64.6 3.3 stack.2
  67.9 7.6 %all-to-all-start.2 = ((bf16[16,160,1280]{2,1,0:T(8,128)(2,1)}), bf16[16,160,1280]{2,1,0:T(8,128)(2,1)}, u32[]{:S(2)}, u32[]{:S(2)}) async-start(bf16[16,160,1280]{2,1,0:T(8,128)(2,1)} %stack.2), calls=%async_computation.2 | async-start | bytes 13107200 | tf_op jit(solution)/shard_map/all_to_all | solution.py:41
  77.0 1.5 fusion.35
  78.5 1.6 convolution_convert_fusion.3
  83.0 118.4 %all-reduce.1 = bf16[1280]{0:T(1024)(128)(2,1)S(1)} all-reduce(bf16[1280]{0:T(1024)(128)(2,1)S(1)} %dynamic-update-slice), channel_id=1, replica_groups=mesh['seq'=16,'dp'=16] {'dp'}, use_global_device_ids=true, to_apply=%add.1 | all-reduce | flops 1280 | bytes 5120
  203.1 2.9 scatter_custom_fusion.2
  206.0 3.9 fusion.31
  210.0 5.1 fusion.1
  215.1 4.7 convolution_convert_fusion.1
  219.8 4.6 convolution_convert_fusion
  224.5 5.2 multiply_reduce_fusion
  229.7 58.0 %reduce-scatter.9.cloned.1.call-done = bf16[80,2560]{1,0:T(8,128)(2,1)} async-done(((bf16[1280,2560]{1,0:T(8,128)(2,1)}), bf16[80,2560]{1,0:T(8,128)(2,1)}) %reduce-scatter.9.cloned.1.call-update) | async-done | bytes 409616 | tf_op jit(solution)/shard_map/reduce_scatter | solution.py:134
  287.7 2.1 copy.80
  291.0 1.7 fusion.8
  293.0 63.5 %reduce-scatter.11.cloned.1.call-done = bf16[160,1280]{1,0:T(8,128)(2,1)} async-done(((bf16[2560,1280]{1,0:T(8,128)(2,1)}), bf16[160,1280]{1,0:T(8,128)(2,1)}) %reduce-scatter.11.cloned.1.call-update) | async-done | bytes 409616 | tf_op jit(solution)/shard_map/reduce_scatter | solution.py:137
  356.5 2.1 copy.82
  361.4 0.9 copy.66
  362.3 75.6 %psum.7 = f32[1280]{0:T(1024)S(1)} all-reduce(f32[1280]{0:T(1024)S(1)} %get-tuple-element.28), channel_id=1, replica_groups=mesh['seq'=16,'dp'=16] {'seq','dp'}, use_global_device_ids=true, to_apply=%region_17.18 | all-reduce | flops 1280 | bytes 10240 | tf_op jit(solution)/shard_map/psum | solution.py:150
  440.1 78.4 %reduce-scatter.15.cloned.1.call-done = bf16[80,160]{1,0:T(8,128)(2,1)} async-done(((bf16[1280,160]{1,0:T(8,128)(2,1)}), bf16[80,160]{1,0:T(8,128)(2,1)}) %reduce-scatter.15.cloned.1.call-update) | async-done | bytes 25616
  (98 shorter events, 17.1 us)
Async XLA Ops:
  7.2 13.6 %copy-start = (bf16[1,192,1280]{2,1,0:T(8,128)(2,1)S(1)}, bf16[1,192,1280]{2,1,0:T(8,128)(2,1)}, u32[]{:S(2)}) copy-start(bf16[1,192,1280]{2,1,0:T(8,128)(2,1)} %param.14) | copy-start | bytes 1474564
  7.2 198.8 %all-gather.2.cloned.1.call-start = ((), (), s32[]{:S(2)}) async-start(), calls=%async_computation.7 | async-start | bytes 6963200 | tf_op jit(solution)/shard_map/all_gather | solution.py:39
  12.1 16.1 %all-to-all-start = ((s32[16,1,32]{2,1,0:T(1,128)}), s32[16,1,32]{2,1,0:T(1,128)S(1)}, u32[]{:S(2)}, u32[]{:S(2)}) async-start(s32[16,1,32]{2,1,0:T(1,128)} %all_to_all.12), calls=%async_computation | async-start | bytes 16384 | tf_op jit(solution)/shard_map/all_to_all | solution.py:69
  28.2 36.3 %copy-start.8 = (bf16[160,1280]{1,0:T(8,128)(2,1)S(1)}, bf16[160,1280]{1,0:T(8,128)(2,1)}, u32[]{:S(2)}) copy-start(bf16[160,1280]{1,0:T(8,128)(2,1)} %param.18) | copy-start | bytes 1228804
  67.9 7.7 %copy-start.9 = (bf16[1,128,1280]{2,1,0:T(8,128)(2,1)S(1)}, bf16[1,128,1280]{2,1,0:T(8,128)(2,1)}, u32[]{:S(2)}) copy-start(bf16[1,128,1280]{2,1,0:T(8,128)(2,1)} %param.11) | copy-start | bytes 983044
  67.9 7.9 %copy-start.10 = (bf16[1,128,1280]{2,1,0:T(8,128)(2,1)S(1)}, bf16[1,128,1280]{2,1,0:T(8,128)(2,1)}, u32[]{:S(2)}) copy-start(bf16[1,128,1280]{2,1,0:T(8,128)(2,1)} %param.12) | copy-start | bytes 983044
  67.9 142.1 %all-to-all-start.2 = ((bf16[16,160,1280]{2,1,0:T(8,128)(2,1)}), bf16[16,160,1280]{2,1,0:T(8,128)(2,1)}, u32[]{:S(2)}, u32[]{:S(2)}) async-start(bf16[16,160,1280]{2,1,0:T(8,128)(2,1)} %stack.2), calls=%async_computation.2 | async-start | bytes 13107200 | tf_op jit(solution)/shard_map/all_to_all | solution.py:41
  75.5 1.0 copy-start.11
  75.5 1.2 copy-start.15
  75.5 212.2 %reduce-scatter.9.cloned.1.call-start = ((), (), s32[]{:S(2)}) async-start(), calls=%async_computation.8 | async-start | bytes 6963200 | tf_op jit(solution)/shard_map/reduce_scatter | solution.py:134
  75.8 2.7 copy-start.3
  76.5 2.0 copy-start.12
  76.7 1.8 copy-start.1
  80.8 1.9 copy-start.16
  80.8 120.6 %copy-start.14 = (bf16[1,128,1280]{2,1,0:T(8,128)(2,1)S(1)}, bf16[1,128,1280]{2,1,0:T(8,128)(2,1)}, u32[]{:S(2)}) copy-start(bf16[1,128,1280]{2,1,0:T(8,128)(2,1)} %param.13) | copy-start | bytes 983044
  219.8 136.7 %reduce-scatter.11.cloned.1.call-start = ((), (), s32[]{:S(2)}) async-start(), calls=%async_computation.9 | async-start | bytes 6963200 | tf_op jit(solution)/shard_map/reduce_scatter | solution.py:137
  224.5 214.1 %reduce-scatter.13.cloned.1.call-start = ((), (), s32[]{:S(2)}) async-start(), calls=%async_computation.10 | async-start | bytes 696320
  289.8 228.7 %reduce-scatter.15.cloned.1.call-start = ((), (), s32[]{:S(2)}) async-start(), calls=%async_computation.11 | async-start | bytes 696320
  289.9 1.0 copy-start.7
  289.9 1.1 copy-start.13
  290.3 2.4 copy-start.5
  291.0 1.7 copy-start.4
  292.7 65.9 %copy-start.2 = (bf16[1,128,1280]{1,2,0:T(8,128)(2,1)S(1)}, bf16[1,128,1280]{1,2,0:T(8,128)(2,1)}, u32[]{:S(2)}) copy-start(bf16[1,128,1280]{1,2,0:T(8,128)(2,1)} %copy-done.1) | copy-start | bytes 983044
  358.6 2.3 copy-start.18
  (2 other events, 1.4 us)
Sparse Core Ops, SparseCore 0:
  10.4 86.2 all-gather.1
  219.9 67.7 reduce-scatter.8
  290.3 66.1 reduce-scatter.10
  359.8 77.1 reduce-scatter.12
  440.3 78.1 reduce-scatter.14
